TPU v7x, 32 devices: a whole 2x2x4 slice. The times are simulated.
32 devices in a mesh: dp: 2 (over x), expert: 16 (over z, y, core).
Axes of the slice: x: 2, y: 2, z: 4, core: 2. Of those that a mesh axis runs over, the one named last changes fastest.
Arguments:
- tokens: bfloat16 [512, 4096], P('expert'), may hold values from -6 to 6
- expert_ids: int32 [512, 8], P('expert'), may hold values from 0 to 15, all different within a row; in each aligned block of 32 rows (0 to 31, 32 to 63, ...) at most 24 rows name the same one
- gate_ints: int32 [512, 8], P('expert'), may hold values from 1 to 1024
- w_gate: bfloat16 [16, 4096, 1536], P('expert', None, 'dp'), may hold values from -0.09375 to 0.09375
- w_up: bfloat16 [16, 4096, 1536], P('expert', None, 'dp'), may hold values from -0.09375 to 0.09375
- w_down: bfloat16 [16, 1536, 4096], P('expert', 'dp'), may hold values from -0.15625 to 0.15625
Outputs:
- mixed: bfloat16 [512, 4096], P('expert')
Inputs may be any that keep to these rules, and one draw needn't show every extreme that they name: `expert_ids`: within the rows of one device each expert is named at most 24 times, and each row names 8 different experts.
All inputs are finite; a program needn't handle non-finite values.
Results may differ from a plain program's by a relative error of at most 0.017.
Values may be sent and summed in bfloat16 or wider, within the bound.
A program may use at most 64 MiB of HBM per device.

v0:
```python
import jax
import jax.numpy as jnp
from jax import lax
from jax.sharding import PartitionSpec as P


def dispatch_form(tokens, expert_ids, gate_ints, w_gate, w_up, w_down):
    tok_rows = tokens.shape[0]
    top_count = expert_ids.shape[1]
    feature = tokens.shape[1]
    groups = lax.axis_size("expert")
    capacity = min(tok_rows, max(2, 3 * tok_rows * top_count // (2 * groups)))
    pairs = tok_rows * top_count
    flat_ids = expert_ids.reshape(pairs)
    onehot = (flat_ids[:, None] == jnp.arange(groups, dtype=jnp.int32)[None, :]).astype(jnp.int32)
    before = jnp.cumsum(onehot, axis=0) - onehot
    slot = jnp.sum(before * onehot, axis=1)
    target = flat_ids * capacity + slot
    select = (jnp.arange(groups * capacity, dtype=jnp.int32)[:, None] == target[None, :]).astype(
        jnp.bfloat16
    )
    owner = (
        (jnp.arange(pairs, dtype=jnp.int32) // top_count)[:, None]
        == jnp.arange(tok_rows, dtype=jnp.int32)[None, :]
    ).astype(jnp.bfloat16)
    placing = jnp.dot(select, owner, preferred_element_type=jnp.float32).astype(jnp.bfloat16)
    outgoing = jnp.dot(placing, tokens, preferred_element_type=jnp.float32).astype(jnp.bfloat16)
    arrived = lax.all_to_all(
        outgoing.reshape(groups, capacity, feature),
        "expert",
        split_axis=0,
        concat_axis=0,
        tiled=True,
    )
    rows = arrived.reshape(groups * capacity, feature)
    gate = jnp.dot(rows, w_gate[0], preferred_element_type=jnp.float32)
    up = jnp.dot(rows, w_up[0], preferred_element_type=jnp.float32)
    hidden = (jax.nn.silu(gate) * up).astype(jnp.bfloat16)
    partial_value = jnp.dot(hidden, w_down[0], preferred_element_type=jnp.float32).astype(
        jnp.bfloat16
    )
    back = lax.all_to_all(
        partial_value.reshape(groups, capacity, feature),
        "expert",
        split_axis=0,
        concat_axis=0,
        tiled=True,
    )
    back_rows = back.reshape(groups * capacity, feature)
    weights = (gate_ints.astype(jnp.float32) / 1024.0)[:, :, None]
    picked = (
        jnp.take(back_rows, target, axis=0)
        .reshape(tok_rows, top_count, feature)
        .astype(jnp.float32)
    )
    local_mix = jnp.sum(weights * picked, axis=1)
    mixed = lax.psum(local_mix.astype(jnp.bfloat16), "dp")
    return mixed


def dense_form(tokens, expert_ids, gate_ints, w_gate, w_up, w_down):
    groups = lax.axis_size("expert")
    me = lax.axis_index("expert")
    chosen = expert_ids[:, :, None] == jnp.arange(groups, dtype=jnp.int32)[None, None, :]
    coef = jnp.sum(jnp.where(chosen, gate_ints[:, :, None], 0), axis=1).astype(jnp.float32) / 1024.0
    rows = lax.all_gather(tokens, "expert", axis=0, tiled=True)
    coefs = lax.all_gather(coef, "expert", axis=0, tiled=True)
    mine = lax.dynamic_slice_in_dim(coefs, me, 1, axis=1)
    gate = jnp.dot(rows, w_gate[0], preferred_element_type=jnp.float32)
    up = jnp.dot(rows, w_up[0], preferred_element_type=jnp.float32)
    hidden = (jax.nn.silu(gate) * up).astype(jnp.bfloat16)
    part = mine * jnp.dot(hidden, w_down[0], preferred_element_type=jnp.float32)
    local = lax.psum_scatter(part.astype(jnp.bfloat16), "expert", scatter_dimension=0, tiled=True)
    return lax.psum(local, "dp")


def on_device(tokens, expert_ids, *rest):
    tok_rows, top_count = expert_ids.shape
    groups = lax.axis_size("expert")
    capacity = min(tok_rows, max(2, 3 * tok_rows * top_count // (2 * groups)))
    form = dense_form if tok_rows <= 2 * capacity else dispatch_form
    return form(tokens, expert_ids, *rest)


def solution(mesh):
    return jax.shard_map(
        on_device,
        mesh=mesh,
        in_specs=(
            P("expert", None),
            P("expert", None),
            P("expert", None),
            P("expert", None, "dp"),
            P("expert", None, "dp"),
            P("expert", "dp", None),
        ),
        out_specs=P("expert", None),
        check_vma=False,
    )
```

profile of v0, /device:TPU:0, one launch (start us, length us, event | category | flops | bytes accessed | tf_op | source)
XLA Modules:
  0.0 190.7 jit_solution(241557817520303641)
XLA Ops:
  6.5 0.0 all-gather.3.cloned.1.call-start
  6.5 0.7 all-gather.3.cloned.1.call-update
  7.3 0.0 reduce-scatter.2.cloned.1.call-start
  7.3 0.7 select_reduce_fusion
  8.0 23.6 %all-gather = f32[16,32,16]{1,2,0:T(8,128)S(1)} all-gather(f32[1,32,16]{1,2,0:T(8,128)S(1)} %multiply_bitcast_fusion), channel_id=1, replica_groups=mesh['dp'=2,'expert'=16] {'expert'}, dimensions={0}, use_global_device_ids=true | all-gather | bytes 34816 | tf_op jit(solution)/shard_map/all_gather | solution.py:67
  31.7 0.1 reshape.3
  31.9 30.9 %all-gather.3.cloned.1.call-done = bf16[512,4096]{1,0:T(8,128)(2,1)} async-done(((bf16[32,4096]{1,0:T(8,128)(2,1)}), bf16[512,4096]{1,0:T(8,128)(2,1)}) %all-gather.3.cloned.1.call-update) | async-done | bytes 4194320 | tf_op jit(solution)/shard_map/all_gather | solution.py:66
  62.8 7.0 %fusion.3 = f32[512,768]{1,0:T(8,128)S(1)} fusion(bf16[512,4096]{1,0:T(8,128)(2,1)} %all-gather.3.cloned.1.call-done, bf16[1,4096,768]{2,1,0:T(8,128)(2,1)} %param.9), kind=kOutput, calls=%fused_computation.4 | convolution fusion | flops 3221225472 | bytes 12058624 | tf_op jit(solution)/shard_map/dot_general | solution.py:69
  69.8 16.6 %multiply_convert_fusion = bf16[512,4096]{1,0:T(8,128)(2,1)} fusion(bf16[1,768,4096]{2,1,0:T(8,128)(2,1)} %param.11, f32[512]{0:T(512)S(1)} %bitcast.20, f32[512,768]{1,0:T(8,128)S(1)} %fusion.3, bf16[512,4096]{1,0:T(8,128)(2,1)} %all-gather.3.cloned.1.call-done, bf16[1,4096,768]{2,1,0:T(8,128)(2,1)} %param.10), kind=kOutput, calls=%fused_computation | convolution fusion | flops 6449004544 | bytes 22546432 | tf_op jit(solution)/shard_map/dot_general | solution.py:72
  86.4 0.0 reduce-scatter.2.cloned.1.call-update
  86.4 0.0 all-reduce.2.cloned.1.call-start
  86.5 71.4 %reduce-scatter.2.cloned.1.call-done = bf16[32,4096]{1,0:T(8,128)(2,1)} async-done(((bf16[512,4096]{1,0:T(8,128)(2,1)}), bf16[32,4096]{1,0:T(8,128)(2,1)}) %reduce-scatter.2.cloned.1.call-update) | async-done | bytes 262160 | tf_op jit(solution)/shard_map/reduce_scatter | solution.py:73
  157.9 0.0 all-reduce.2.cloned.1.call-update
  157.9 24.6 %all-reduce.2.cloned.1.call-done = bf16[32,4096]{1,0:T(8,128)(2,1)} async-done(((bf16[32,4096]{1,0:T(8,128)(2,1)}), bf16[32,4096]{1,0:T(8,128)(2,1)}) %all-reduce.2.cloned.1.call-update) | async-done | bytes 262160 | tf_op jit(solution)/shard_map/psum | solution.py:74
  182.5 1.7 copy.18
  (3 shorter events, 0.1 us)
Async XLA Ops:
  6.5 56.3 %all-gather.3.cloned.1.call-start = ((), (), s32[]{:S(2)}) async-start(), calls=%async_computation.1 | async-start | bytes 4456448 | tf_op jit(solution)/shard_map/all_gather | solution.py:66
  7.3 150.6 %reduce-scatter.2.cloned.1.call-start = ((), (), s32[]{:S(2)}) async-start(), calls=%async_computation.2 | async-start | bytes 4456448 | tf_op jit(solution)/shard_map/reduce_scatter | solution.py:73
  86.4 96.1 %all-reduce.2.cloned.1.call-start = ((), (), s32[]{:S(2)}) async-start(), calls=%async_computation.3 | async-start | bytes 524288 | tf_op jit(solution)/shard_map/psum | solution.py:74
Sparse Core Ops, SparseCore 0:
  9.5 53.2 all-gather.2
  86.6 71.2 reduce-scatter.1
  160.2 22.2 all-reduce.1
where the time goes:
time: 191 us
  waiting for transfers between devices  128 us (67%)
  blocking collectives  23.6 us (12%)
  matrix products  23.6 us (12%)
  between operations  13.1 us (7%)
    reduce_scatter x1, waiting for transfers between devices, dense_form(): lax.psum_scatter(part.astype(jnp.bfloat16), 'expert', scatter_dimension=0...  71.4 us
    all_gather x1, waiting for transfers between devices, dense_form(): rows = lax.all_gather(tokens, 'expert', axis=0, tiled=True)  30.9 us
    psum x1, waiting for transfers between devices, dense_form(): return lax.psum(local, 'dp')  24.6 us
    all_gather x1, blocking collectives, dense_form(): coefs = lax.all_gather(coef, 'expert', axis=0, tiled=True)  23.6 us
    dot_general x1, matrix products, dense_form(): part = mine * jnp.dot(hidden, w_down[0], preferred_element_type=jnp.float32)  16.6 us
    dot_general x1, matrix products, dense_form(): gate = jnp.dot(rows, w_gate[0], preferred_element_type=jnp.float32)  7.03 us
  transfers between devices with their start and end apart: 3, of which 3 were waited for; matrix products, arithmetic and copies ran while one was open for 0% of the time, Pallas kernels for 0%

commit v1 on v0

--- a/solution.py
+++ b/solution.py
@@ -63,8 +63,12 @@
     me = lax.axis_index("expert")
     chosen = expert_ids[:, :, None] == jnp.arange(groups, dtype=jnp.int32)[None, None, :]
     coef = jnp.sum(jnp.where(chosen, gate_ints[:, :, None], 0), axis=1).astype(jnp.float32) / 1024.0
-    rows = lax.all_gather(tokens, "expert", axis=0, tiled=True)
-    coefs = lax.all_gather(coef, "expert", axis=0, tiled=True)
+    use_view = lambda inputs, u_in: jnp.split(
+        lax.all_gather(jnp.concatenate([inputs, u_in], axis=1), "expert", axis=0, tiled=True),
+        [inputs.shape[1]],
+        axis=1,
+    )
+    rows, coefs = use_view(tokens, coef)
     mine = lax.dynamic_slice_in_dim(coefs, me, 1, axis=1)
     gate = jnp.dot(rows, w_gate[0], preferred_element_type=jnp.float32)
     up = jnp.dot(rows, w_up[0], preferred_element_type=jnp.float32)

time: 191 us -> 220 us (1.15)
  waiting for transfers between devices: 128 us -> 175 us
  blocking collectives: 23.6 us -> 0 us
    all_gather x1, waiting for transfers between devices: 30.9 us -> 79 us  [dense_form(): lax.all_gather(jnp.concatenate([inputs, u_in], axis=1), 'expert', axis=0,...]
    all_gather x1 -> x0, blocking collectives: 23.6 us -> none  [dense_form(): coefs = lax.all_gather(coef, 'expert', axis=0, tiled=True)]
where the time goes in v1:
time: 220 us; the launch traced here: 219 us
  waiting for transfers between devices  175 us (80%)
  matrix products  25.5 us (12%)
  between operations  13.1 us (6%)
  local copies, waits for them, and re-layouts  2.95 us (1%)
  other arithmetic  2.59 us (1%)
    all_gather x1, waiting for transfers between devices, dense_form(): lax.all_gather(jnp.concatenate([inputs, u_in], axis=1), 'expert', axis=0,...  79 us
    reduce_scatter x1, waiting for transfers between devices, dense_form(): lax.psum_scatter(part.astype(jnp.bfloat16), 'expert', scatter_dimension=0...  71.4 us
    psum x1, waiting for transfers between devices, dense_form(): return lax.psum(local, 'dp')  24.6 us
    dot_general x1, matrix products, dense_form(): part = mine * jnp.dot(hidden, w_down[0], preferred_element_type=jnp.float32)  17.8 us
    dot_general x1, matrix products, dense_form(): gate = jnp.dot(rows, w_gate[0], preferred_element_type=jnp.float32)  7.68 us
  transfers between devices with their start and end apart: 3, of which 3 were waited for; matrix products, arithmetic and copies ran while one was open for 0% of the time, Pallas kernels for 0%

profile of v1, /device:TPU:0, one launch (start us, length us, event | category | flops | bytes accessed | tf_op | source)
XLA Modules:
  0.0 219.3 jit_solution(799332968160529200)
XLA Ops:
  6.5 0.0 all-gather.2.cloned.1.call-start
  6.5 0.7 select_reduce_fusion
  7.3 0.1 copy.11
  7.3 1.0 convert_element_type.12
  8.3 0.9 pad_maximum_fusion
  9.2 0.0 all-gather.2.cloned.1.call-update
  9.2 0.0 reduce-scatter.2.cloned.1.call-start
  9.3 79.0 %all-gather.2.cloned.1.call-done = f32[512,4112]{1,0:T(8,128)} async-done(((f32[32,4112]{1,0:T(8,128)}), f32[512,4112]{1,0:T(8,128)}) %all-gather.2.cloned.1.call-update) | async-done | bytes 8421392 | tf_op jit(solution)/shard_map/all_gather | solution.py:67
  88.3 1.0 split.8
  89.3 0.2 dynamic-slice_reduce_fusion
  89.5 7.7 %fusion.2 = f32[512,768]{1,0:T(8,128)S(1)} fusion(f32[512,4112]{1,0:T(8,128)} %all-gather.2.cloned.1.call-done, bf16[1,4096,768]{2,1,0:T(8,128)(2,1)} %param.9), kind=kOutput, calls=%fused_computation.3 | convolution fusion | flops 3221225472 | bytes 12058624 | tf_op jit(solution)/shard_map/dot_general | solution.py:73
  97.2 17.8 %multiply_convert_fusion = bf16[512,4096]{1,0:T(8,128)(2,1)} fusion(bf16[1,768,4096]{2,1,0:T(8,128)(2,1)} %param.11, f32[512]{0:T(512)S(1)} %dynamic-slice_reduce_fusion, f32[512,768]{1,0:T(8,128)S(1)} %fusion.2, bf16[1,4096,768]{2,1,0:T(8,128)(2,1)} %param.10, f32[512,4112]{1,0:T(8,128)} %all-gather.2.cloned.1.call-done), kind=kOutput, calls=%fused_computation | convolution fusion | flops 6449004544 | bytes 22546432 | tf_op jit(solution)/shard_map/dot_general | solution.py:76
  115.0 0.0 reduce-scatter.2.cloned.1.call-update
  115.0 0.0 all-reduce.2.cloned.1.call-start
  115.1 71.4 %reduce-scatter.2.cloned.1.call-done = bf16[32,4096]{1,0:T(8,128)(2,1)} async-done(((bf16[512,4096]{1,0:T(8,128)(2,1)}), bf16[32,4096]{1,0:T(8,128)(2,1)}) %reduce-scatter.2.cloned.1.call-update) | async-done | bytes 262160 | tf_op jit(solution)/shard_map/reduce_scatter | solution.py:77
  186.5 0.0 all-reduce.2.cloned.1.call-update
  186.5 24.6 %all-reduce.2.cloned.1.call-done = bf16[32,4096]{1,0:T(8,128)(2,1)} async-done(((bf16[32,4096]{1,0:T(8,128)(2,1)}), bf16[32,4096]{1,0:T(8,128)(2,1)}) %all-reduce.2.cloned.1.call-update) | async-done | bytes 262160 | tf_op jit(solution)/shard_map/psum | solution.py:78
  211.1 1.7 copy.13
  (1 shorter events, 0.0 us)
Async XLA Ops:
  6.5 81.8 %all-gather.2.cloned.1.call-start = ((), (), s32[]{:S(2)}) async-start(), calls=%async_computation.1 | async-start | bytes 9191424 | tf_op jit(solution)/shard_map/all_gather | solution.py:67
  9.2 177.3 %reduce-scatter.2.cloned.1.call-start = ((), (), s32[]{:S(2)}) async-start(), calls=%async_computation.2 | async-start | bytes 4456448 | tf_op jit(solution)/shard_map/reduce_scatter | solution.py:77
  115.0 96.1 %all-reduce.2.cloned.1.call-start = ((), (), s32[]{:S(2)}) async-start(), calls=%async_computation.3 | async-start | bytes 524288 | tf_op jit(solution)/shard_map/psum | solution.py:78
Sparse Core Ops, SparseCore 0:
  9.6 78.6 all-gather.1
  115.1 71.2 reduce-scatter.1
  188.8 22.3 all-reduce.1

commit v2 on v0

--- a/solution.py
+++ b/solution.py
@@ -1,7 +1,16 @@
+import functools
 import jax
 import jax.numpy as jnp
 from jax import lax
 from jax.sharding import PartitionSpec as P
+
+
+def get_the_teams(here_x, across):
+    all_rows = jnp.sum(jax.lax.all_gather(here_x, across), axis=0)
+    return all_rows
+
+
+grid_pair = functools.partial(get_the_teams, across="dp")
 
 
 def dispatch_form(tokens, expert_ids, gate_ints, w_gate, w_up, w_down):
@@ -71,7 +80,7 @@
     hidden = (jax.nn.silu(gate) * up).astype(jnp.bfloat16)
     part = mine * jnp.dot(hidden, w_down[0], preferred_element_type=jnp.float32)
     local = lax.psum_scatter(part.astype(jnp.bfloat16), "expert", scatter_dimension=0, tiled=True)
-    return lax.psum(local, "dp")
+    return grid_pair(local)
 
 
 def on_device(tokens, expert_ids, *rest):

time: 191 us -> 173 us (0.906)
  waiting for transfers between devices: 128 us -> 103 us
  blocking collectives: 23.6 us -> 31 us
    psum x1 -> x0, waiting for transfers between devices: 24.6 us -> none  [dense_form(): return lax.psum(local, 'dp')]
    all_gather x0 -> x1, blocking collectives: none -> 7.39 us  [get_the_teams(): all_rows = jnp.sum(jax.lax.all_gather(here_x, across), axis=0)]
  transfers between devices with their start and end apart: 3 -> 2, of which waited for: 3 -> 2; matrix products, arithmetic and copies ran while one was open for 0% -> 1% of each run, Pallas kernels for 0% -> 0%
where the time goes in v2:
time: 173 us
  waiting for transfers between devices  103 us (60%)
  blocking collectives  31 us (18%)
  matrix products  23.6 us (14%)
  between operations  13.4 us (8%)
    reduce_scatter x1, waiting for transfers between devices, dense_form(): lax.psum_scatter(part.astype(jnp.bfloat16), 'expert', scatter_dimension=0...  71.5 us
    all_gather x1, waiting for transfers between devices, dense_form(): rows = lax.all_gather(tokens, 'expert', axis=0, tiled=True)  30.9 us
    all_gather x1, blocking collectives, dense_form(): coefs = lax.all_gather(coef, 'expert', axis=0, tiled=True)  23.6 us
    dot_general x1, matrix products, dense_form(): part = mine * jnp.dot(hidden, w_down[0], preferred_element_type=jnp.float32)  16.6 us
    all_gather x1, blocking collectives, get_the_teams(): all_rows = jnp.sum(jax.lax.all_gather(here_x, across), axis=0)  7.39 us
    dot_general x1, matrix products, dense_form(): gate = jnp.dot(rows, w_gate[0], preferred_element_type=jnp.float32)  7.03 us
  transfers between devices with their start and end apart: 2, of which 2 were waited for; matrix products, arithmetic and copies ran while one was open for 1% of the time, Pallas kernels for 0%

profile of v2, /device:TPU:0, one launch (start us, length us, event | category | flops | bytes accessed | tf_op | source)
XLA Modules:
  0.0 173.0 jit_solution(10782803829590468985)
XLA Ops:
  6.5 0.0 all-gather.4.cloned.1.call-start
  6.5 0.7 all-gather.4.cloned.1.call-update
  7.3 0.0 reduce-scatter.2.cloned.1.call-start
  7.3 0.7 select_reduce_fusion
  8.0 23.6 %all-gather.1 = f32[16,32,16]{1,2,0:T(8,128)S(1)} all-gather(f32[1,32,16]{1,2,0:T(8,128)S(1)} %multiply_bitcast_fusion), channel_id=1, replica_groups=mesh['dp'=2,'expert'=16] {'expert'}, dimensions={0}, use_global_device_ids=true | all-gather | bytes 34816 | tf_op jit(solution)/shard_map/all_gather | solution.py:76
  31.7 0.1 reshape.4
  31.9 30.9 %all-gather.4.cloned.1.call-done = bf16[512,4096]{1,0:T(8,128)(2,1)} async-done(((bf16[32,4096]{1,0:T(8,128)(2,1)}), bf16[512,4096]{1,0:T(8,128)(2,1)}) %all-gather.4.cloned.1.call-update) | async-done | bytes 4194320 | tf_op jit(solution)/shard_map/all_gather | solution.py:75
  62.8 7.0 %fusion.3 = f32[512,768]{1,0:T(8,128)S(1)} fusion(bf16[512,4096]{1,0:T(8,128)(2,1)} %all-gather.4.cloned.1.call-done, bf16[1,4096,768]{2,1,0:T(8,128)(2,1)} %param.9), kind=kOutput, calls=%fused_computation.4 | convolution fusion | flops 3221225472 | bytes 12058624 | tf_op jit(solution)/shard_map/dot_general | solution.py:78
  69.8 16.6 %multiply_convert_fusion = bf16[512,4096]{1,0:T(8,128)(2,1)} fusion(bf16[1,768,4096]{2,1,0:T(8,128)(2,1)} %param.11, f32[512]{0:T(512)S(1)} %bitcast.22, f32[512,768]{1,0:T(8,128)S(1)} %fusion.3, bf16[512,4096]{1,0:T(8,128)(2,1)} %all-gather.4.cloned.1.call-done, bf16[1,4096,768]{2,1,0:T(8,128)(2,1)} %param.10), kind=kOutput, calls=%fused_computation | convolution fusion | flops 6449004544 | bytes 22546432 | tf_op jit(solution)/shard_map/dot_general | solution.py:81
  86.4 0.0 reduce-scatter.2.cloned.1.call-update
  86.4 71.5 %reduce-scatter.2.cloned.1.call-done = bf16[32,4096]{1,0:T(8,128)(2,1)} async-done(((bf16[512,4096]{1,0:T(8,128)(2,1)}), bf16[32,4096]{1,0:T(8,128)(2,1)}) %reduce-scatter.2.cloned.1.call-update) | async-done | bytes 262160 | tf_op jit(solution)/shard_map/reduce_scatter | solution.py:82
  157.9 7.4 %all-gather = bf16[64,4096]{1,0:T(8,128)(2,1)S(1)} all-gather(bf16[32,4096]{1,0:T(8,128)(2,1)} %reduce-scatter.2.cloned.1.call-done), channel_id=2, replica_groups=mesh['dp'=2,'expert'=16] {'dp'}, dimensions={0}, use_global_device_ids=true | all-gather | bytes 786432 | tf_op jit(solution)/shard_map/all_gather | solution.py:9
  165.3 0.8 reduce_sum.22
  (3 shorter events, 0.1 us)
Async XLA Ops:
  6.5 56.3 %all-gather.4.cloned.1.call-start = ((), (), s32[]{:S(2)}) async-start(), calls=%async_computation.1 | async-start | bytes 4456448 | tf_op jit(solution)/shard_map/all_gather | solution.py:75
  7.3 150.6 %reduce-scatter.2.cloned.1.call-start = ((), (), s32[]{:S(2)}) async-start(), calls=%async_computation.2 | async-start | bytes 4456448 | tf_op jit(solution)/shard_map/reduce_scatter | solution.py:82
Sparse Core Ops, SparseCore 0:
  9.5 53.2 all-gather.3
  86.5 71.2 reduce-scatter.1
